TPU v7x, 32 devices: a whole 2x2x4 slice. The times are simulated.
32 devices in a mesh: groups: 2 (over y), seq: 8 (over z, x), cache: 2 (over core).
Axes of the slice: x: 2, y: 2, z: 4, core: 2. Of those that a mesh axis runs over, the one named last changes fastest.
Arguments:
- queries: bfloat16 [128, 2048, 128], P('groups', ('seq', 'cache')), parts along dimension 0, may hold values from -8 to 8
- stretch_keys: bfloat16 [128, 2048, 128], P('groups', 'seq'), parts along dimension 0, may hold values from -8 to 8
- stretch_values: bfloat16 [128, 2048, 128], P('groups', 'seq'), parts along dimension 0, may hold values from -6 to 6
- cache_keys: bfloat16 [128, 2048, 128], P(('groups', 'seq'), 'cache'), parts along dimension 0, may hold values from -6 to 6
- cache_values: bfloat16 [128, 2048, 128], P(('groups', 'seq'), 'cache'), parts along dimension 0, may hold values from -6 to 6
- rand_blocks: int32 [32, 3], P('groups'), parts along dimension 0, may hold values from 2 to 28, as said below
Outputs:
- attended: bfloat16 [128, 2048, 128], P('groups', ('seq', 'cache')), parts along dimension 0
There are 2 independent parts, one for each index of `groups`. A program takes and returns all parts, laid end to end along the dimension named above; each array names one. Nothing has to cross between parts.
Inputs may be any that keep to these rules, and one draw needn't show every extreme that they name: `rand_blocks`: row i holds 3 different block numbers, each at least 2 and below 16 + i - 2.
All inputs are finite; a program needn't handle non-finite values.
Results may differ from a plain program's by a relative error of at most 0.0049.
Values may be sent and summed in bfloat16 or wider, within the bound.
A program may use at most 128 MiB of HBM per device.

v0:
```python
import functools
import math

import jax
import jax.numpy as jnp
from jax import lax
from jax.experimental import pallas as pl
from jax.experimental.pallas import tpu as pltpu
from jax.sharding import PartitionSpec as P

BLK = 128
CB = 16
LINE = 2
HIDDEN = -1e30
MESH = pl.DeviceIdType.MESH


def fused_kernel(
    chips, pairs, split, rand_ref, q_hbm, k_hbm, v_hbm, ck_hbm, cv_hbm, out_hbm, *scratch
):
    helped = chips // 2 // LINE * split
    take = iter(scratch)
    q_bufs, k_bufs, v_bufs, o_bufs = ([next(take) for _ in range(pairs)] for _ in range(4))
    hq_bufs, hk_bufs, hv_bufs, ho_bufs = ([next(take) for _ in range(helped)] for _ in range(4))
    l_bufs = [next(take) for _ in range(split)]
    hl_buf, part_a, part_b, lse_a, lse_b, merged = (next(take) for _ in range(6))
    q_in, k_in, v_in, hq_in, hk_in, hv_in = (next(take) for _ in range(6))
    (
        q_out, k_out, v_out, ks_out, vs_out, ck_out, cv_out, o_out, o_in, low_in,
        hk_out, hv_out, hq_out, hq_down, l_out, ho_out, hl_out,
        a_in, b_in, la_in, lb_in, m_out,
    ) = (next(take) for _ in range(22))

    s = lax.axis_index("seq")
    c = lax.axis_index("cache")
    per_device = q_hbm.shape[1]
    per_chip = k_hbm.shape[1]
    side_blocks = ck_hbm.shape[1]
    cached = 2 * side_blocks
    head_width = q_hbm.shape[3]
    mine = 2 * s + c
    devices = 2 * chips
    middle = chips // 2
    half_blocks = middle * per_chip
    upper = s // middle
    own_first = cached + upper * half_blocks
    helper = middle - LINE + upper * LINE
    is_helper = (s >= middle - LINE) & (s < middle + LINE)

    barrier = pltpu.get_barrier_semaphore()

    def greet(d, carry):
        other = (mine + d) % devices
        pl.semaphore_signal(
            barrier,
            inc=1,
            device_id={"seq": other // 2, "cache": other % 2},
            device_id_type=MESH,
        )
        return carry

    lax.fori_loop(1, devices, greet, 0)
    pl.semaphore_wait(barrier, devices - 1)

    def remote(src, dst, send, recv, s2, c2):
        pltpu.make_async_remote_copy(
            src_ref=src,
            dst_ref=dst,
            send_sem=send,
            recv_sem=recv,
            device_id={"seq": s2, "cache": c2},
            device_id_type=MESH,
        ).start()

    def local(src, dst, sem):
        pltpu.make_async_copy(src, dst, sem).start()

    def await_bytes(ref, sem):
        pltpu.make_async_copy(ref, ref, sem).wait()

    stretch_at = pl.ds(cached + s * per_chip, per_chip)
    query_at = pl.ds(mine * per_device, per_device)
    half_at = pl.ds((s % middle) * per_chip, per_chip)

    def spread(p):
        def queries_to(s2):
            same = (2 * s2 + c) * pairs + p
            cross = (2 * s2 + 1 - c) * pairs + p
            remote(q_hbm.at[same], q_bufs[p].at[query_at], q_out, q_in.at[p], s2, c)
            remote(q_hbm.at[cross], q_bufs[p].at[query_at], q_out, q_in.at[p], s2, 1 - c)

        def keys_to(s2, k_sem, v_sem):
            same = (2 * s2 + c) * pairs + p
            remote(k_hbm.at[same], k_bufs[p].at[stretch_at], k_sem, k_in.at[p], s2, c)
            remote(v_hbm.at[same], v_bufs[p].at[stretch_at], v_sem, v_in.at[p], s2, c)

        if p < split:

            def to_half(d, carry):
                keys_to(upper * middle + (s + d) % middle, ks_out, vs_out)
                return carry

            def to_chip(d, carry):
                queries_to((s + d) % chips)
                return carry

            lax.fori_loop(1, chips, to_chip, 0)
            lax.fori_loop(1, middle, to_half, 0)
        else:

            def to_chip(d, carry):
                s2 = (s + d) % chips
                keys_to(s2, k_out, v_out)
                queries_to(s2)
                return carry

            lax.fori_loop(1, chips, to_chip, 0)
        own = mine * pairs + p
        cross = (2 * s + 1 - c) * pairs + p
        side = pl.ds(c * side_blocks, side_blocks)
        give = (1 - c) * pairs + p
        keep = c * pairs + p
        remote(ck_hbm.at[give], k_bufs[p].at[side], ck_out, k_in.at[p], s, 1 - c)
        remote(cv_hbm.at[give], v_bufs[p].at[side], cv_out, v_in.at[p], s, 1 - c)
        remote(q_hbm.at[cross], q_bufs[p].at[query_at], q_out, q_in.at[p], s, 1 - c)
        local(q_hbm.at[own], q_bufs[p].at[query_at], q_in.at[p])
        local(k_hbm.at[own], k_bufs[p].at[stretch_at], k_in.at[p])
        local(v_hbm.at[own], v_bufs[p].at[stretch_at], v_in.at[p])
        local(ck_hbm.at[keep], k_bufs[p].at[side], k_in.at[p])
        local(cv_hbm.at[keep], v_bufs[p].at[side], v_in.at[p])

    def head_of(side_upper, x, side, u):
        home = (1 - side_upper) * middle + (u // split) * LINE + x
        return (2 * home + side) * pairs + u % split

    def spread_help(u):
        for x in range(LINE):
            target = helper + x
            away = s != target
            for side in range(2):
                head = head_of(upper, x, side, u)

                @pl.when(away | (c != side))
                def _():
                    remote(q_hbm.at[head], hq_bufs[u].at[query_at], hq_out, hq_in.at[u], target, side)

                @pl.when(jnp.logical_not(away) & (c == side))
                def _():
                    local(q_hbm.at[head], hq_bufs[u].at[query_at], hq_in.at[u])

                @pl.when(upper == 1)
                def _():
                    remote(
                        q_hbm.at[head_of(0, x, side, u)],
                        hq_bufs[u].at[query_at],
                        hq_down,
                        hq_in.at[u],
                        middle - LINE + x,
                        side,
                    )

            same = head_of(upper, x, c, u)

            @pl.when(away)
            def _():
                remote(k_hbm.at[same], hk_bufs[u].at[half_at], hk_out, hk_in.at[u], target, c)
                remote(v_hbm.at[same], hv_bufs[u].at[half_at], hv_out, hv_in.at[u], target, c)

            @pl.when(jnp.logical_not(away))
            def _():
                local(k_hbm.at[same], hk_bufs[u].at[half_at], hk_in.at[u])
                local(v_hbm.at[same], hv_bufs[u].at[half_at], hv_in.at[u])

    factor = math.log2(math.e) / math.sqrt(head_width)
    row_at = lax.broadcasted_iota(jnp.int32, (BLK, BLK), 0)
    col_at = lax.broadcasted_iota(jnp.int32, (BLK, BLK), 1)
    later = col_at > row_at

    def joined(tiles):
        return tiles.reshape(-1, head_width)

    def softmax_sum(query, keys_of, values_of, shown):
        scores = [
            lax.dot_general(
                query, tile, (((1,), (1,)), ((), ())), preferred_element_type=jnp.float32
            )
            for tile in keys_of()
        ]
        scores[0] = jnp.where(later, HIDDEN, scores[0])
        if shown is not None:
            scores = [
                score if show is None else jnp.where(show, score, HIDDEN)
                for score, show in zip(scores, shown)
            ]
        top = functools.reduce(
            jnp.maximum, [jnp.max(score, axis=1, keepdims=True) for score in scores]
        )
        weights = [jnp.exp2((score - top) * factor) for score in scores]
        total = sum(jnp.sum(weight, axis=1, keepdims=True) for weight in weights)
        result = sum(
            jnp.dot(weight.astype(jnp.bfloat16), tile, preferred_element_type=jnp.float32)
            for weight, tile in zip(weights, values_of())
        )
        return (result / total).astype(jnp.bfloat16), top * factor + jnp.log2(total)

    def attend(p, i):
        def listed(buffer):
            first = cached + i
            tiles = [buffer[first], joined(buffer[pl.ds(first - 2, 2)]), joined(buffer[0:2])]
            return tiles + [buffer[rand_ref[i, n]] for n in range(rand_ref.shape[1])]

        result, _ = softmax_sum(
            q_bufs[p][i], lambda: listed(k_bufs[p]), lambda: listed(v_bufs[p]), None
        )
        o_bufs[p][i] = result

    def in_half(b):
        return (b >= own_first) & (b < own_first + half_blocks)

    def as_rows(lse):
        return jnp.broadcast_to(lse, (BLK, BLK)).T[0:1]

    def attend_home(p, i):
        numbers = [cached + i, cached + i - 2, cached + i - 1]
        numbers += [rand_ref[i, n] for n in range(rand_ref.shape[1])]
        shown = [(b < cached) | in_half(b) for b in numbers]
        places = [jnp.where(show, b, 0) for show, b in zip(shown, numbers)]

        def listed(buffer):
            return [buffer[place] for place in places] + [joined(buffer[0:2])]

        result, lse = softmax_sum(
            q_bufs[p][i],
            lambda: listed(k_bufs[p]),
            lambda: listed(v_bufs[p]),
            shown + [None],
        )
        o_bufs[p][i] = result
        l_bufs[p][i] = as_rows(lse)

    def attend_help(u, i):
        numbers = [cached + i, cached + i - 2, cached + i - 1]
        numbers += [rand_ref[i, n] for n in range(rand_ref.shape[1])]
        shown = [in_half(b) for b in numbers]
        places = [jnp.where(show, b - own_first, 0) for show, b in zip(shown, numbers)]

        def listed(buffer):
            return [buffer[place] for place in places]

        result, lse = softmax_sum(
            hq_bufs[u][i], lambda: listed(hk_bufs[u]), lambda: listed(hv_bufs[u]), shown
        )
        ho_bufs[u][i] = result
        hl_buf[u, i] = as_rows(lse)

    def each_block(target, act):
        def block_step(n, inner):
            act(target * per_device + n)
            return inner

        lax.fori_loop(0, per_device, block_step, 0)

    def blocks_at(target):
        return pl.ds(target * per_device, per_device)

    def put(src, dst, send, recv, target):
        @pl.when(target != mine)
        def _():
            remote(src, dst, send, recv, target // 2, target % 2)

        @pl.when(target == mine)
        def _():
            local(src, dst, recv)

    def direct_head(p):
        await_bytes(q_bufs[p], q_in.at[p])
        await_bytes(k_bufs[p], k_in.at[p])
        await_bytes(v_bufs[p], v_in.at[p])
        head = mine * pairs + p

        def device_step(d, carry):
            target = (mine + d) % devices
            each_block(target, lambda i: attend(p, i))
            put(o_bufs[p].at[blocks_at(target)], out_hbm.at[head], o_out, o_in, target)
            return carry

        lax.fori_loop(1, devices + 1, device_step, 0)

    def split_head(p):
        came = cached + half_blocks
        await_bytes(q_bufs[p], q_in.at[p])
        await_bytes(k_bufs[p].at[pl.ds(0, came)], k_in.at[p])
        await_bytes(v_bufs[p].at[pl.ds(0, came)], v_in.at[p])
        head = mine * pairs + p
        place = mine * split + p

        def device_step(d, carry):
            target = (mine + d) % devices
            whole = (upper == 0) & (target < chips)
            each_block(target, lambda i: attend_home(p, i))

            @pl.when(whole)
            def _():
                put(o_bufs[p].at[blocks_at(target)], out_hbm.at[head], o_out, low_in, target)

            @pl.when(jnp.logical_not(whole))
            def _():
                put(o_bufs[p].at[blocks_at(target)], part_a.at[place], o_out, a_in, target)
                put(l_bufs[p].at[blocks_at(target)], lse_a.at[place], l_out, la_in, target)

            return carry

        lax.fori_loop(1, devices + 1, device_step, 0)

    def help_head(u):
        @pl.when(upper == 0)
        def _():
            await_bytes(hq_bufs[u], hq_in.at[u])

        @pl.when(upper == 1)
        def _():
            await_bytes(hq_bufs[u].at[pl.ds(0, half_blocks)], hq_in.at[u])

        await_bytes(hk_bufs[u], hk_in.at[u])
        await_bytes(hv_bufs[u], hv_in.at[u])
        home = (1 - upper) * middle + (u // split) * LINE + (s - helper)
        place = (2 * home + c) * split + u % split

        def serve(target):
            each_block(target, lambda i: attend_help(u, i))
            put(ho_bufs[u].at[blocks_at(target)], part_b.at[place], ho_out, b_in, target)
            put(hl_buf.at[u, blocks_at(target)], lse_b.at[place], hl_out, lb_in, target)

        def device_step(d, carry):
            target = (mine + d) % devices

            @pl.when((upper == 0) | (target >= chips))
            def _():
                serve(target)

            return carry

        lax.fori_loop(1, devices + 1, device_step, 0)

    places = devices * split

    def merge():
        def waits(n):
            await_bytes(part_a.at[pl.ds(0, n)], a_in)
            await_bytes(part_b.at[pl.ds(0, n)], b_in)
            await_bytes(lse_a.at[pl.ds(0, n)], la_in)
            await_bytes(lse_b.at[pl.ds(0, n)], lb_in)

        def blend(place, carry):
            for n in range(per_device):

                def spread_out(ref):
                    return jnp.broadcast_to(ref[place, n], (BLK, BLK)).T

                left, right = spread_out(lse_a), spread_out(lse_b)
                top = jnp.maximum(left, right)
                left, right = jnp.exp2(left - top), jnp.exp2(right - top)
                both = part_a[place, n].astype(jnp.float32) * left
                both += part_b[place, n].astype(jnp.float32) * right
                merged[place, n] = (both / (left + right)).astype(jnp.bfloat16)
            local(
                merged.at[place], out_hbm.at[place // split * pairs + place % split], m_out
            )
            return carry

        @pl.when(upper == 0)
        def _():
            waits(places // 2)
            lax.fori_loop(places // 2, places, blend, 0)

        @pl.when(upper == 1)
        def _():
            waits(places)
            lax.fori_loop(0, places, blend, 0)

    def help_all():
        @pl.when(is_helper)
        def _():
            for u in range(helped):
                help_head(u)

    def spread_helps():
        for u in range(helped):
            spread_help(u)

    order = [(lambda p=p: spread(p), lambda p=p: split_head(p)) for p in range(split)]
    order.append((spread_helps, help_all))
    order += [(lambda p=p: spread(p), lambda p=p: direct_head(p)) for p in range(split, pairs)]
    ahead = 3
    for send, _ in order[:ahead]:
        send()
    for n, (_, work) in enumerate(order):
        if n + ahead < len(order):
            order[n + ahead][0]()
        work()
    merge()

    def blocks(n):
        return q_hbm.at[pl.ds(0, n)]

    def chunks(n):
        return k_hbm.at[pl.ds(0, n)]

    others = devices - 1
    await_bytes(out_hbm.at[pl.ds(0, devices * (pairs - split))], o_in)
    await_bytes(blocks(others * pairs), q_out)
    await_bytes(blocks(others * pairs), o_out)
    await_bytes(chunks((chips - 1) * (pairs - split)), k_out)
    await_bytes(chunks((chips - 1) * (pairs - split)), v_out)
    await_bytes(chunks((middle - 1) * split), ks_out)
    await_bytes(chunks((middle - 1) * split), vs_out)
    await_bytes(ck_hbm.at[pl.ds(0, pairs)], ck_out)
    await_bytes(cv_hbm.at[pl.ds(0, pairs)], cv_out)

    @pl.when(is_helper)
    def _():
        await_bytes(chunks((LINE - 1) * helped), hk_out)
        await_bytes(chunks((LINE - 1) * helped), hv_out)
        await_bytes(blocks((2 * LINE - 1) * helped), hq_out)

        @pl.when(upper == 0)
        def _():
            await_bytes(chunks(others * helped // 2), ho_out)
            await_bytes(hl_buf.at[:, pl.ds(0, others * per_device)], hl_out)

        @pl.when(upper == 1)
        def _():
            await_bytes(chunks((chips - 1) * helped // 2), ho_out)
            await_bytes(hl_buf.at[:, pl.ds(0, (chips - 1) * per_device)], hl_out)

    @pl.when(jnp.logical_not(is_helper))
    def _():
        await_bytes(chunks(LINE * helped), hk_out)
        await_bytes(chunks(LINE * helped), hv_out)
        await_bytes(blocks(2 * LINE * helped), hq_out)

    @pl.when(upper == 0)
    def _():
        await_bytes(blocks(chips * split), low_in)
        await_bytes(merged.at[pl.ds(0, places // 2)], m_out)
        await_bytes(lse_a.at[pl.ds(0, chips * split)], l_out)

    @pl.when(upper == 1)
    def _():
        await_bytes(blocks(2 * LINE * helped), hq_down)
        await_bytes(merged, m_out)
        await_bytes(lse_a.at[pl.ds(0, others * split)], l_out)


def heads_apart(queries, stretch_keys, stretch_values, cache_keys, cache_values, rand_blocks):
    chips = lax.axis_size("seq")
    pairs = cache_keys.shape[0] // 2
    split = pairs // 2
    helped = chips // 2 // LINE * split
    per_device = queries.shape[1] // BLK
    length = 2 * chips * queries.shape[1]
    keys = 2 * cache_keys.shape[1] + length
    width = queries.shape[2]

    def blocked(array):
        return array.reshape(array.shape[0], -1, BLK, width)

    def buffer(size, count):
        return [pltpu.VMEM((size // BLK, BLK, width), jnp.bfloat16)] * count

    places = 2 * chips * split
    part = pltpu.VMEM((places, per_device, BLK, width), jnp.bfloat16)
    lse = pltpu.VMEM((places, per_device, 1, BLK), jnp.float32)
    buffers = buffer(length, pairs) + buffer(keys, 2 * pairs) + buffer(length, pairs)
    buffers += buffer(length, helped) + buffer(length // 2, 2 * helped) + buffer(length, helped)
    buffers += [pltpu.VMEM((length // BLK, 1, BLK), jnp.float32)] * split
    buffers += [pltpu.VMEM((helped, length // BLK, 1, BLK), jnp.float32)]
    buffers += [part, part, lse, lse, part]
    anywhere = pl.BlockSpec(memory_space=pl.ANY)
    attended = pl.pallas_call(
        functools.partial(fused_kernel, chips, pairs, split),
        out_shape=jax.ShapeDtypeStruct(blocked(queries).shape, queries.dtype),
        in_specs=[pl.BlockSpec(memory_space=pltpu.SMEM)] + [anywhere] * 5,
        out_specs=anywhere,
        scratch_shapes=buffers
        + [pltpu.SemaphoreType.DMA((pairs,))] * 3
        + [pltpu.SemaphoreType.DMA((helped,))] * 3
        + [pltpu.SemaphoreType.DMA(())] * 22,
        compiler_params=pltpu.CompilerParams(collective_id=0, has_side_effects=True),
    )(
        rand_blocks,
        blocked(queries),
        blocked(stretch_keys),
        blocked(stretch_values),
        blocked(cache_keys),
        blocked(cache_values),
    )
    return attended.reshape(queries.shape)


def block_lists(rand_blocks):
    block_count = rand_blocks.shape[0]
    starts = jnp.arange(block_count, dtype=jnp.int32)[:, None] + CB
    window = starts + jnp.array([-2, -1, 0], jnp.int32)[None, :]
    anchors = jnp.broadcast_to(jnp.array([0, 1], jnp.int32)[None, :], (block_count, 2))
    return jnp.concatenate([window, anchors, rand_blocks], axis=1)


def attend_blocks(query_blocks, key_lists, key_blocks, value_blocks):
    groups, block_width, head_width = query_blocks.shape
    listed = key_lists.shape[1]
    chosen_keys = jnp.take(key_blocks, key_lists, axis=0).reshape(
        groups, listed * block_width, head_width
    )
    chosen_values = jnp.take(value_blocks, key_lists, axis=0).reshape(
        groups, listed * block_width, head_width
    )
    scores = jnp.einsum(
        "gqd,gkd->gqk", query_blocks, chosen_keys, preferred_element_type=jnp.float32
    )
    scores = scores * (1.0 / math.sqrt(head_width))
    key_slot = jnp.arange(listed * block_width, dtype=jnp.int32)
    query_slot = jnp.arange(block_width, dtype=jnp.int32)
    blocked = (key_slot // block_width == 2)[None, :] & (
        (key_slot % block_width)[None, :] > query_slot[:, None]
    )
    scores = jnp.where(blocked[None], -jnp.inf, scores)
    row_max = jnp.max(scores, axis=2, keepdims=True)
    weights = jnp.exp(scores - row_max)
    row_probs = (weights / jnp.sum(weights, axis=2, keepdims=True)).astype(jnp.bfloat16)
    result = jnp.einsum(
        "gqk,gkd->gqd", row_probs, chosen_values, preferred_element_type=jnp.float32
    )
    return result.astype(jnp.bfloat16)


def rows_apart(queries, stretch_keys, stretch_values, cache_keys, cache_values, rand_blocks):
    local_rows = queries.shape[1]
    head_width = queries.shape[2]
    seq_devices = lax.axis_size("seq")
    cache_devices = lax.axis_size("cache")
    cache_side = lax.axis_index("cache")
    query_heads, key_heads, value_heads = (
        lax.all_to_all(queries, "seq", split_axis=0, concat_axis=1, tiled=True),
        lax.all_to_all(stretch_keys, "seq", split_axis=0, concat_axis=1, tiled=True),
        lax.all_to_all(stretch_values, "seq", split_axis=0, concat_axis=1, tiled=True),
    )
    prefix_keys, prefix_values = (
        lax.all_gather(cache_keys, "cache", axis=1, tiled=True),
        lax.all_gather(cache_values, "cache", axis=1, tiled=True),
    )
    all_lists = block_lists(rand_blocks)
    per_segment = local_rows // BLK
    my_blocks = seq_devices * per_segment
    block_order = jnp.arange(my_blocks, dtype=jnp.int32)
    global_block = (
        block_order // per_segment * cache_devices + cache_side
    ) * per_segment + block_order % per_segment
    my_lists = jnp.take(all_lists, global_block, axis=0)
    group_size = math.gcd(my_blocks, max(1, 2048 // BLK))
    group_count = my_blocks // group_size
    lists_grouped = my_lists.reshape(group_count, group_size, my_lists.shape[1])

    def one_pair(operands):
        query_rows, key_rows, value_rows, prefix_key, prefix_value = operands
        key_blocks = jnp.concatenate([prefix_key, key_rows], axis=0).reshape(-1, BLK, head_width)
        value_blocks = jnp.concatenate([prefix_value, value_rows], axis=0).reshape(
            -1, BLK, head_width
        )
        query_groups = query_rows.reshape(group_count, group_size, BLK, head_width)

        def one_group(group_operands):
            query_group, list_group = group_operands
            return attend_blocks(query_group, list_group, key_blocks, value_blocks)

        result = lax.map(one_group, (query_groups, lists_grouped))
        return result.reshape(my_blocks * BLK, head_width)

    attended_heads = lax.map(
        one_pair, (query_heads, key_heads, value_heads, prefix_keys, prefix_values)
    )
    return lax.all_to_all(attended_heads, "seq", split_axis=1, concat_axis=0, tiled=True)


def per_device(queries, stretch_keys, stretch_values, cache_keys, cache_values, rand_blocks):
    if cache_keys.shape[0] % 4 == 0 and lax.axis_size("seq") % (2 * LINE) == 0:
        plan = heads_apart
    else:
        plan = rows_apart
    return plan(queries, stretch_keys, stretch_values, cache_keys, cache_values, rand_blocks)


def solution(mesh):
    placed = (
        P("groups", ("seq", "cache"), None),
        P("groups", "seq", None),
        P("groups", "seq", None),
        P(("groups", "seq"), "cache", None),
        P(("groups", "seq"), "cache", None),
        P("groups", None),
    )
    return jax.shard_map(
        per_device,
        mesh=mesh,
        in_specs=placed,
        out_specs=P("groups", ("seq", "cache"), None),
        check_vma=False,
    )
```

profile of v0, /device:TPU:11, one launch (start us, length us, event | category | flops | bytes accessed | tf_op | source)
XLA Modules:
  0.0 173.5 jit_solution(13447720058130138457)
XLA Ops:
  0.0 1.4 copy.7.rand_ref
  1.4 169.0 %shard_map.64 = bf16[64,1,128,128]{3,2,1,0:T(8,128)(2,1)} custom-call(s32[16,3]{1,0:T(8,128)} %copy.7.rand_ref, bf16[64,1,128,128]{3,2,1,0:T(8,128)(2,1)} %bitcast.9, bf16[64,2,128,128]{3,2,1,0:T(8,128)(2,1)} %bitcast.7, bf16[64,2,128,128]{3,2,1,0:T(8,128)(2,1)} %bitcast.8, bf16[8,8,128,128]{3,2,1,0:T(8,128)(2,1)} %bitcast.10, bf16[8,8,128,128]{3,2,1,0:T(8,128)(2,1)} %bitcast.11), custom_call_target="tpu_custom_call" | custom-call | tf_op jit(solution)/shard_map/pallas_call | solution.py:480
  170.3 3.2 %copy.9 = bf16[64,128,128]{2,1,0:T(8,128)(2,1)} copy(bf16[64,128,128]{2,1,0:T(8,128)(2,1)} %bitcast.6) | data formatting | bytes 4194304
where the time goes:
time: 174 us
  Pallas kernels  169 us (97%)
  local copies, waits for them, and re-layouts  4.51 us (3%)
    pallas_call x1, Pallas kernels, heads_apart(): pl.pallas_call(functools.partial(fused_kernel, chips, pairs, split), out_...  169 us
    unnamed x2, local copies, waits for them, and re-layouts  4.51 us

commit v1 on v0

--- a/solution.py
+++ b/solution.py
@@ -207,7 +207,7 @@
         def listed(buffer):
             first = cached + i
             tiles = [buffer[first], joined(buffer[pl.ds(first - 2, 2)]), joined(buffer[0:2])]
-            return tiles + [buffer[rand_ref[i, n]] for n in range(rand_ref.shape[1])]
+            return tiles + [buffer[rand_ref[n, i]] for n in range(rand_ref.shape[0])]
 
         result, _ = softmax_sum(
             q_bufs[p][i], lambda: listed(k_bufs[p]), lambda: listed(v_bufs[p]), None
@@ -222,7 +222,7 @@
 
     def attend_home(p, i):
         numbers = [cached + i, cached + i - 2, cached + i - 1]
-        numbers += [rand_ref[i, n] for n in range(rand_ref.shape[1])]
+        numbers += [rand_ref[n, i] for n in range(rand_ref.shape[0])]
         shown = [(b < cached) | in_half(b) for b in numbers]
         places = [jnp.where(show, b, 0) for show, b in zip(shown, numbers)]
 
@@ -240,7 +240,7 @@
 
     def attend_help(u, i):
         numbers = [cached + i, cached + i - 2, cached + i - 1]
-        numbers += [rand_ref[i, n] for n in range(rand_ref.shape[1])]
+        numbers += [rand_ref[n, i] for n in range(rand_ref.shape[0])]
         shown = [in_half(b) for b in numbers]
         places = [jnp.where(show, b - own_first, 0) for show, b in zip(shown, numbers)]
 
@@ -488,7 +488,7 @@
         + [pltpu.SemaphoreType.DMA(())] * 22,
         compiler_params=pltpu.CompilerParams(collective_id=0, has_side_effects=True),
     )(
-        rand_blocks,
+        rand_blocks.T,
         blocked(queries),
         blocked(stretch_keys),
         blocked(stretch_values),

time: 174 us -> 172 us (0.989)
    unnamed x2 -> x1, local copies, waits for them, and re-layouts: 4.51 us -> 3.16 us
where the time goes in v1:
time: 172 us
  Pallas kernels  169 us (98%)
  local copies, waits for them, and re-layouts  3.16 us (2%)
    pallas_call x1, Pallas kernels, heads_apart(): pl.pallas_call(functools.partial(fused_kernel, chips, pairs, split), out_...  169 us

profile of v1, /device:TPU:11, one launch (start us, length us, event | category | flops | bytes accessed | tf_op | source)
XLA Modules:
  0.0 172.0 jit_solution(6898777748402236071)
XLA Ops:
  0.0 168.9 %shard_map.64 = bf16[64,1,128,128]{3,2,1,0:T(8,128)(2,1)} custom-call(s32[3,16]{1,0:T(4,128)} %bitcast.13, bf16[64,1,128,128]{3,2,1,0:T(8,128)(2,1)} %bitcast.10, bf16[64,2,128,128]{3,2,1,0:T(8,128)(2,1)} %bitcast.8, bf16[64,2,128,128]{3,2,1,0:T(8,128)(2,1)} %bitcast.9, bf16[8,8,128,128]{3,2,1,0:T(8,128)(2,1)} %bitcast.11, bf16[8,8,128,128]{3,2,1,0:T(8,128)(2,1)} %bitcast.12), custom_call_target="tpu_custom_call" | custom-call | tf_op jit(solution)/shard_map/pallas_call | solution.py:480
  168.9 3.2 %copy.8 = bf16[64,128,128]{2,1,0:T(8,128)(2,1)} copy(bf16[64,128,128]{2,1,0:T(8,128)(2,1)} %bitcast.7) | data formatting | bytes 4194304
